TPU v7x, 32 devices: a whole 2x2x4 slice. The times are simulated.
32 devices in a mesh: dom: 8 (over z, x), bud: 4 (over y, core).
Axes of the slice: x: 2, y: 2, z: 4, core: 2. Of those that a mesh axis runs over, the one named last changes fastest.
Arguments:
- right_side: float32 [3, 32, 64, 128], P(None, 'dom', 'bud'), may hold values from -8 to 8
- stiffness: float32 [32, 64, 128], P('dom', 'bud'), may hold values from 0.5 to 2
- coupling: float32 [27, 3, 3], replicated, may hold values from -2 to 3, as said below
- iterate_in: float32 [3, 32, 64, 128], P(None, 'dom', 'bud'), may hold values from -8 to 8
- residual_in: float32 [3, 32, 64, 128], P(None, 'dom', 'bud'), may hold values from -20 to 20
- direction_in: float32 [3, 32, 64, 128], P(None, 'dom', 'bud'), may hold values from -20 to 20
- backup_in: float32 [2, 3, 32, 64, 128], P(None, None, 'dom', 'bud'), may hold values from -8 to 8
- beta_prev: float32 [1], replicated, may hold values from 0.3 to 0.9
- fail_column: int32 [8], P('dom'), may hold values from 0 to 3, as said below
- buddy_bit: int32 [8], P('dom'), may hold values from 0 to 1
Outputs:
- iterate: float32 [3, 32, 64, 128], P(None, 'dom', 'bud')
- residual: float32 [3, 32, 64, 128], P(None, 'dom', 'bud')
- backup: float32 [2, 3, 32, 64, 128], P(None, None, 'dom', 'bud')
Inputs may be any that keep to these rules, and one draw needn't show every extreme that they name: `fail_column`: every column index appears among the lost columns. The buddy of block (i, k) is the block (i, k with binary digit buddy_bit[i] flipped). coupling[26 - o] is the transpose of coupling[o]; each diagonal entry of coupling[13] exceeds 1.02 times the sum of the magnitudes of all other entries of its row over all 27 blocks.
All inputs are finite; a program needn't handle non-finite values.
Results may differ from a plain program's by a relative error of at most 0.00015.
Values sent between devices are 32-bit elements; how exact they have to be, the bound alone decides.
A program may use at most 64 MiB of HBM per device.

v0:
```python
import functools

import jax
import jax.numpy as jnp
from jax import lax
from jax.experimental import pallas as pl
from jax.experimental.pallas import tpu as pltpu
from jax.sharding import PartitionSpec as P

SWEEPS = 4
LOW = 0.01
HIGH = 1.99
SIDES = [(sx, sy) for sx in (-1, 0, 1) for sy in (-1, 0, 1) if (sx, sy) != (0, 0)]
Y0 = 8


def kernel(
    nd, nb, levels,
    rhs, stiff, cpl, x_in, r_in, p_in, bk, beta, fc, bb,
    x_out, r_out, b_out,
    pads, padl, flat, ysend, yrecv, csend, crecv, saved, bsend, brecv,
    r0, inv, img, target, solved, update,
    red, red2, rrecv, brecv2,
    hs, hr, ss, sr, bs, br, d1s, d1r, d2s, d2r,
):
    nx, ny, nz = stiff.shape
    step = 2 if nx % 2 == 0 else 1
    dom, bud = lax.axis_index("dom"), lax.axis_index("bud")

    def has(side):
        sx, sy = side
        ok = None
        for cond in (
            ([dom > 0] if sx < 0 else [dom < nd - 1] if sx > 0 else [])
            + ([bud > 0] if sy < 0 else [bud < nb - 1] if sy > 0 else [])
        ):
            ok = cond if ok is None else jnp.logical_and(ok, cond)
        return ok

    def remote(src, dst, send, recv, d, b):
        return pltpu.make_async_remote_copy(
            src_ref=src, dst_ref=dst, send_sem=send, recv_sem=recv,
            device_id={"dom": d, "bud": b}, device_id_type=pl.DeviceIdType.MESH,
        )

    def flip(level):
        stride = 1 << level
        return bud + stride * (1 - 2 * (lax.rem(bud // stride, 2)))

    pads[...] = jnp.zeros(pads.shape, pads.dtype)
    padl[...] = jnp.zeros(padl.shape, padl.dtype)
    yrecv[...] = jnp.zeros(yrecv.shape, yrecv.dtype)
    crecv[...] = jnp.zeros(crecv.shape, crecv.dtype)

    barrier = pltpu.get_barrier_semaphore()

    def greet(d, b):
        pl.semaphore_signal(
            barrier, inc=1, device_id={"dom": d, "bud": b},
            device_id_type=pl.DeviceIdType.MESH,
        )

    for j in range(1, nb):
        greet(dom, lax.rem(bud + j, nb))
    for j in range(1, nd):
        greet(lax.rem(dom + j, nd), bud)
    diagonals = [s for s in SIDES if s[0] != 0 and s[1] != 0]
    for side in diagonals:
        @pl.when(has(side))
        def _(side=side):
            greet(dom + side[0], bud + side[1])

    me_failed = jnp.full((1, ny, nz), fc[0], jnp.int32) == bud
    bit_here = jnp.full((1, ny, nz), bb[0], jnp.int32)

    def halo_copies(e, which, side):
        sx, sy = side
        i = SIDES.index(side)
        o = SIDES.index((-sx, -sy))
        to = (dom + sx, bud + sy)
        if sy == 0:
            src = flat.at[e, :, nx - 1 if sx > 0 else 0]
            dst = pads.at[e, :, 0 if sx > 0 else nx + 1, pl.ds(Y0, ny), :]
        elif sx == 0:
            src = ysend.at[e, 1 if sy > 0 else 0]
            dst = yrecv.at[e, 0 if sy > 0 else 1]
        else:
            src = csend.at[e, i]
            dst = crecv.at[e, o]
        return remote(src, dst, hs.at[e, i], hr.at[e, o], *to)

    def landing(e, side):
        sx, sy = side
        i = SIDES.index(side)
        if sy == 0:
            src = flat.at[e, :, nx - 1 if sx > 0 else 0]
            dst = pads.at[e, :, nx + 1 if sx > 0 else 0, pl.ds(Y0, ny), :]
        elif sx == 0:
            src = ysend.at[e, 1 if sy > 0 else 0]
            dst = yrecv.at[e, 1 if sy > 0 else 0]
        else:
            src = csend.at[e, i]
            dst = crecv.at[e, i]
        return remote(src, dst, hs.at[e, i], hr.at[e, i], dom + sx, bud + sy)

    def pack(e):
        for c in range(3):
            for x in range(nx):
                row = c * nx + x
                ysend[e, 0, row:row + 1, :] = flat[e, c, x, 0:1, :]
                ysend[e, 1, row:row + 1, :] = flat[e, c, x, ny - 1:ny, :]
            for i, (sx, sy) in enumerate(SIDES):
                if sx != 0 and sy != 0:
                    y = ny - 1 if sy > 0 else 0
                    csend[e, i, c:c + 1, :] = flat[e, c, nx - 1 if sx > 0 else 0, y:y + 1, :]

    def send_halo(e):
        for side in SIDES:
            @pl.when(has(side))
            def _(side=side):
                halo_copies(e, 0, side).start()

    def take_halo(e):
        for side in SIDES:
            @pl.when(has(side))
            def _(side=side):
                landing(e, side).wait_recv()
        for c in range(3):
            for x in range(nx):
                row = c * nx + x
                pads[e, c, x + 1, Y0 - 1:Y0, :] = yrecv[e, 0, row:row + 1, :]
                pads[e, c, x + 1, Y0 + ny:Y0 + ny + 1, :] = yrecv[e, 1, row:row + 1, :]
            for i, (sx, sy) in enumerate(SIDES):
                if sx != 0 and sy != 0:
                    y = Y0 + ny if sy > 0 else Y0 - 1
                    pads[e, c, nx + 1 if sx > 0 else 0, y:y + 1, :] = crecv[e, i, c:c + 1, :]

    def end_halo(e):
        for side in SIDES:
            @pl.when(has(side))
            def _(side=side):
                halo_copies(e, 0, side).wait_send()

    lane = lax.broadcasted_iota(jnp.int32, (step, ny, nz), 2)

    def apply(pad, out):
        @pl.loop(0, nx // step)
        def _(j):
            x = j * step
            acc = [[None] * 3 for _ in range(3)]
            for dx in range(3):
                for dy in range(3):
                    for b in range(3):
                        w = pad[b, pl.ds(x + dx, step), Y0 - 1 + dy:Y0 - 1 + dy + ny, :]
                        for dz in range(3):
                            o = (dx * 3 + dy) * 3 + dz
                            for a in range(3):
                                term = cpl[o * 9 + a * 3 + b] * w
                                acc[dz][a] = term if acc[dz][a] is None else acc[dz][a] + term
            for a in range(3):
                before = jnp.where(lane == 0, 0.0, pltpu.roll(acc[0][a], 1, 2))
                after = jnp.where(lane == nz - 1, 0.0, pltpu.roll(acc[2][a], nz - 1, 2))
                out[a, pl.ds(x, step)] = acc[1][a] + before + after

    centre = [cpl[13 * 9 + a * 3 + a] for a in range(3)]

    for a in range(3):
        scaled = jnp.where(me_failed, 0.0, x_in[a] * stiff[...])
        flat[0, a] = scaled
        pads[0, a, 1:nx + 1, Y0:Y0 + ny, :] = scaled
        inv[a] = 1.0 / (stiff[...] * stiff[...] * centre[a])
    pack(0)

    beside_x = jnp.where(dom > 0, 1, 0) + jnp.where(dom < nd - 1, 1, 0)
    beside_y = jnp.where(bud > 0, 1, 0) + jnp.where(bud < nb - 1, 1, 0)
    pl.semaphore_wait(barrier, nb - 1 + nd - 1 + beside_x * beside_y)

    fetch = [[remote(bk.at[w], saved.at[l, w], ss.at[l, w], sr.at[l, w], dom, flip(l))
              for l in range(levels)] for w in range(2)]
    for l in range(levels):
        fetch[1][l].start()
    send_halo(0)
    for l in range(levels):
        fetch[0][l].start()

    keep = [[remote(bsend.at[w], brecv.at[l, w], bs.at[l, w], br.at[l, w], dom, flip(l))
             for l in range(levels)] for w in range(3)]

    def pick(buf, w, a):
        value = buf[0, w, a]
        for l in range(1, levels):
            value = jnp.where(bit_here == l, buf[l, w, a], value)
        return value

    for l in range(levels):
        fetch[1][l].wait_recv()
    for a in range(3):
        p0 = jnp.where(me_failed, pick(saved, 1, a), p_in[a])
        bsend[0, a] = p0
        u0 = p0 * stiff[...]
        flat[1, a] = u0
        pads[1, a, 1:nx + 1, Y0:Y0 + ny, :] = u0
    pack(1)
    send_halo(1)
    for l in range(levels):
        fetch[0][l].wait_recv()
    for a in range(3):
        restored_z = pick(saved, 1, a) - beta[0] * pick(saved, 0, a)
        restored_r = restored_z * (stiff[...] * stiff[...] * centre[a])
        z0 = jnp.where(me_failed, restored_z, inv[a] * r_in[a])
        r0[a] = jnp.where(me_failed, restored_r, r_in[a])
        target[a] = rhs[a] - restored_r
        bsend[1, a] = z0
        a0 = z0 * stiff[...]
        flat[2, a] = a0
        pads[2, a, 1:nx + 1, Y0:Y0 + ny, :] = a0
    pack(2)
    send_halo(2)
    for l in range(levels):
        keep[0][l].start()
    for l in range(levels):
        keep[1][l].start()

    take_halo(1)
    apply(pads.at[1], img.at[0])
    for a in range(3):
        b0 = img[0, a] * (1.0 / jnp.full((1, ny, nz), centre[a], jnp.float32))
        flat[3, a] = b0
        pads[3, a, 1:nx + 1, Y0:Y0 + ny, :] = b0
    pack(3)
    send_halo(3)
    for a in range(3):
        bsend[2, a] = flat[3, a] / stiff[...]
    for l in range(levels):
        keep[2][l].start()

    take_halo(2)
    apply(pads.at[2], img.at[1])
    take_halo(0)
    apply(pads.at[0], img.at[3])
    take_halo(3)
    apply(pads.at[3], img.at[2])

    def dot(*terms):
        total = None
        for a in range(3):
            for v in terms:
                t = v(a)
                total = t if total is None else total + t
        return jnp.sum(jnp.sum(total, axis=0), axis=0, keepdims=True)

    red[...] = jnp.zeros(red.shape, red.dtype)
    red[0:1, :] = dot(lambda a: r0[a] * bsend[1, a])
    red[1:2, :] = dot(lambda a: flat[1, a] * img[0, a])
    red[2:3, :] = dot(lambda a: flat[2, a] * img[0, a])
    red[3:4, :] = dot(lambda a: flat[3, a] * img[0, a])
    red[4:5, :] = dot(lambda a: flat[2, a] * img[1, a])
    red[5:6, :] = dot(lambda a: flat[3, a] * img[1, a])
    red[6:7, :] = dot(lambda a: flat[3, a] * img[2, a])

    first = [remote(red, rrecv.at[j - 1], d1s.at[j - 1], d1r.at[j - 1], lax.rem(dom + j, nd), bud)
             for j in range(1, nd)]
    for c in first:
        c.start()

    centre_value = (HIGH + LOW) / 2.0
    half_width = (HIGH - LOW) / 2.0
    ratio_value = centre_value / half_width
    weight = 1.0 / ratio_value
    for a in range(3):
        t = target[a] - img[3, a] * stiff[...]
        d = inv[a] * t / centre_value
        target[a] = t
        update[a] = d
        solved[a] = d
        padl[a, 1:nx + 1, Y0:Y0 + ny, :] = d * stiff[...]
    for sweep in range(SWEEPS - 1):
        apply(padl, img.at[3])
        weight_next = 1.0 / (2.0 * ratio_value - weight)
        for a in range(3):
            remain = target[a] - img[3, a] * stiff[...]
            d = weight_next * weight * update[a] + (2.0 * weight_next / half_width) * (inv[a] * remain)
            y = solved[a] + d
            update[a] = d
            solved[a] = y
            if sweep < SWEEPS - 2:
                padl[a, 1:nx + 1, Y0:Y0 + ny, :] = y * stiff[...]
        weight = weight_next

    for c in first:
        c.wait_recv()
    total = red[...]
    for j in range(nd - 1):
        total = total + rrecv[j]
    red2[...] = total
    second = [remote(red2, brecv2.at[j - 1], d2s.at[j - 1], d2r.at[j - 1], dom, lax.rem(bud + j, nb))
              for j in range(1, nb)]
    for c in second:
        c.start()
    for w in range(3):
        for l in range(levels):
            keep[w][l].wait_recv()
    for a in range(3):
        b_out[0, a] = pick(brecv, 0, a)
    for c in second:
        c.wait_recv()
    total = red2[...]
    for j in range(nb - 1):
        total = total + brecv2[j]
    sums = jnp.sum(total, axis=1, keepdims=True)
    g0, c0, e0, f0, h0, h1, h2 = [jnp.broadcast_to(sums[j:j + 1], (1, nz)) for j in range(7)]
    alpha0 = g0 / c0
    g1 = g0 - 2.0 * alpha0 * e0 + alpha0 * alpha0 * f0
    beta0 = g1 / g0
    c1 = (
        h0 - 2.0 * alpha0 * h1 + alpha0 * alpha0 * h2
        + 2.0 * beta0 * (e0 - alpha0 * f0) + beta0 * beta0 * c0
    )
    alpha1 = g1 / c1
    alpha0, beta0, alpha1 = alpha0[None], beta0[None], alpha1[None]
    for a in range(3):
        p0 = bsend[0, a]
        p1 = bsend[1, a] - alpha0 * bsend[2, a] + beta0 * p0
        x0 = jnp.where(me_failed, solved[a], x_in[a])
        x_out[a] = x0 + alpha0 * p0 + alpha1 * p1
        t0 = img[0, a]
        q1 = img[1, a] - alpha0 * img[2, a] + beta0 * t0
        r_out[a] = r0[a] - stiff[...] * (alpha0 * t0 + alpha1 * q1)
        b_out[1, a] = (
            pick(brecv, 1, a) - alpha0 * pick(brecv, 2, a) + beta0 * pick(brecv, 0, a)
        )

    for e in range(4):
        end_halo(e)
    for w in range(2):
        for l in range(levels):
            fetch[w][l].wait_send()
    for w in range(3):
        for l in range(levels):
            keep[w][l].wait_send()
    for c in first + second:
        c.wait_send()


def on_device(nd, nb, rhs, stiff, coupling, x_in, r_in, p_in, backup_in, beta, fc, bb):
    levels = nb.bit_length() - 1
    nx, ny, nz = stiff.shape
    f32 = jnp.float32
    rows = -(-3 * nx // 8) * 8
    vmem = pl.BlockSpec(memory_space=pltpu.VMEM)
    smem = pl.BlockSpec(memory_space=pltpu.SMEM)
    field = (3, nx, ny, nz)
    dma = pltpu.SemaphoreType.DMA
    return pl.pallas_call(
        functools.partial(kernel, nd, nb, levels),
        out_shape=(
            jax.ShapeDtypeStruct(field, f32),
            jax.ShapeDtypeStruct(field, f32),
            jax.ShapeDtypeStruct((2,) + field, f32),
        ),
        in_specs=[vmem, vmem, smem, vmem, vmem, vmem, vmem, smem, smem, smem],
        out_specs=(vmem, vmem, vmem),
        scratch_shapes=[
            pltpu.VMEM((4, 3, nx + 2, ny + 2 * Y0, nz), f32),
            pltpu.VMEM((3, nx + 2, ny + 2 * Y0, nz), f32),
            pltpu.VMEM((4,) + field, f32),
            pltpu.VMEM((4, 2, rows, nz), f32),
            pltpu.VMEM((4, 2, rows, nz), f32),
            pltpu.VMEM((4, 8, 8, nz), f32),
            pltpu.VMEM((4, 8, 8, nz), f32),
            pltpu.VMEM((levels, 2) + field, f32),
            pltpu.VMEM((3,) + field, f32),
            pltpu.VMEM((levels, 3) + field, f32),
            pltpu.VMEM(field, f32),
            pltpu.VMEM(field, f32),
            pltpu.VMEM((4,) + field, f32),
            pltpu.VMEM(field, f32),
            pltpu.VMEM(field, f32),
            pltpu.VMEM(field, f32),
            pltpu.VMEM((8, nz), f32),
            pltpu.VMEM((8, nz), f32),
            pltpu.VMEM((nd - 1, 8, nz), f32),
            pltpu.VMEM((nb - 1, 8, nz), f32),
            dma((4, 8)), dma((4, 8)),
            dma((levels, 2)), dma((levels, 2)),
            dma((levels, 3)), dma((levels, 3)),
            dma((nd - 1,)), dma((nd - 1,)),
            dma((nb - 1,)), dma((nb - 1,)),
        ],
        compiler_params=pltpu.CompilerParams(
            collective_id=0, has_side_effects=True, vmem_limit_bytes=40 * 1024 * 1024
        ),
    )(rhs, stiff, coupling.reshape(-1), x_in, r_in, p_in, backup_in, beta, fc, bb)


def solution(mesh):
    nd, nb = mesh.shape["dom"], mesh.shape["bud"]
    placed = (
        P(None, "dom", "bud", None),
        P("dom", "bud", None),
        P(),
        P(None, "dom", "bud", None),
        P(None, "dom", "bud", None),
        P(None, "dom", "bud", None),
        P(None, None, "dom", "bud", None),
        P(),
        P("dom"),
        P("dom"),
    )
    return jax.shard_map(
        functools.partial(on_device, nd, nb),
        mesh=mesh,
        in_specs=placed,
        out_specs=(
            P(None, "dom", "bud", None),
            P(None, "dom", "bud", None),
            P(None, None, "dom", "bud", None),
        ),
        check_vma=False,
    )
```

profile of v0, /device:TPU:0, one launch (start us, length us, event | category | flops | bytes accessed | tf_op | source)
XLA Modules:
  0.0 36.6 jit_solution(6859494870873560525)
XLA Ops:
  0.6 0.0 copy-start.1
  2.6 0.8 %copy.13 = f32[27,3,3]{2,1,0:T(4,128)S(1)} copy(f32[27,3,3]{0,2,1:T(4,128)} %param.12) | data formatting | bytes 1944 | tf_op args[2]
  3.4 0.2 reshape.9.cpl
  3.6 0.0 copy-done.1
  3.6 0.0 copy-start
  3.6 0.9 %copy-done = f32[2,3,4,16,128]{4,3,2,1,0:T(8,128)S(1)} copy-done((f32[2,3,4,16,128]{4,3,2,1,0:T(8,128)S(1)}, f32[2,3,4,16,128]{4,3,2,1,0:T(8,128)}, u32[]{:S(2)}) %copy-start) | copy-done | bytes 196632
  4.5 0.0 copy-start.2
  4.5 0.9 %copy-done.2 = f32[3,4,16,128]{3,2,1,0:T(8,128)S(1)} copy-done((f32[3,4,16,128]{3,2,1,0:T(8,128)S(1)}, f32[3,4,16,128]{3,2,1,0:T(8,128)}, u32[]{:S(2)}) %copy-start.2) | copy-done | bytes 98328
  5.4 0.0 copy-start.3
  5.4 0.9 %copy-done.3 = f32[3,4,16,128]{3,2,1,0:T(8,128)S(1)} copy-done((f32[3,4,16,128]{3,2,1,0:T(8,128)S(1)}, f32[3,4,16,128]{3,2,1,0:T(8,128)}, u32[]{:S(2)}) %copy-start.3) | copy-done | bytes 98328
  6.3 0.0 copy-start.4
  6.3 0.9 %copy-done.4 = f32[3,4,16,128]{3,2,1,0:T(8,128)S(1)} copy-done((f32[3,4,16,128]{3,2,1,0:T(8,128)S(1)}, f32[3,4,16,128]{3,2,1,0:T(8,128)}, u32[]{:S(2)}) %copy-start.4) | copy-done | bytes 98328
  7.2 0.0 copy-start.5
  7.2 0.8 %copy-done.5 = f32[4,16,128]{2,1,0:T(8,128)S(1)} copy-done((f32[4,16,128]{2,1,0:T(8,128)S(1)}, f32[4,16,128]{2,1,0:T(8,128)}, u32[]{:S(2)}) %copy-start.5) | copy-done | bytes 32792
  8.0 26.7 %shard_map.121 = (f32[3,4,16,128]{3,2,1,0:T(8,128)S(1)}, f32[3,4,16,128]{3,2,1,0:T(8,128)S(1)}, f32[2,3,4,16,128]{4,3,2,1,0:T(8,128)S(1)}) custom-call(f32[3,4,16,128]{3,2,1,0:T(8,128)S(1)} %copy-done.1, f32[4,16,128]{2,1,0:T(8,128)S(1)} %copy-done.5, f32[243]{0:T(256)S(1)} %reshape.9.cpl, f32[3,4,16,128]{3,2,1,0:T(8,128)S(1)} %copy-done.2, ...), custom_call_target="tpu_custom_call" | custom-call | tf_op jit(solution)/shard_map/pallas_call | solution.py:354
  34.6 0.6 %copy.20 = f32[3,4,16,128]{3,2,1,0:T(8,128)} copy(f32[3,4,16,128]{3,2,1,0:T(8,128)S(1)} %get-tuple-element.6) | data formatting | bytes 196608
  35.3 0.6 %copy.21 = f32[3,4,16,128]{3,2,1,0:T(8,128)} copy(f32[3,4,16,128]{3,2,1,0:T(8,128)S(1)} %get-tuple-element.7) | data formatting | bytes 196608
  35.9 0.7 %copy.22 = f32[2,3,4,16,128]{4,3,2,1,0:T(8,128)} copy(f32[2,3,4,16,128]{4,3,2,1,0:T(8,128)S(1)} %get-tuple-element.8) | data formatting | bytes 393216
Async XLA Ops:
  0.6 3.0 %copy-start.1 = (f32[3,4,16,128]{3,2,1,0:T(8,128)S(1)}, f32[3,4,16,128]{3,2,1,0:T(8,128)}, u32[]{:S(2)}) copy-start(f32[3,4,16,128]{3,2,1,0:T(8,128)} %rhs.1) | copy-start | bytes 294916
  3.6 0.9 %copy-start = (f32[2,3,4,16,128]{4,3,2,1,0:T(8,128)S(1)}, f32[2,3,4,16,128]{4,3,2,1,0:T(8,128)}, u32[]{:S(2)}) copy-start(f32[2,3,4,16,128]{4,3,2,1,0:T(8,128)} %bk.1) | copy-start | bytes 589828
  4.5 0.9 %copy-start.2 = (f32[3,4,16,128]{3,2,1,0:T(8,128)S(1)}, f32[3,4,16,128]{3,2,1,0:T(8,128)}, u32[]{:S(2)}) copy-start(f32[3,4,16,128]{3,2,1,0:T(8,128)} %x_in.1) | copy-start | bytes 294916
  5.4 0.9 %copy-start.3 = (f32[3,4,16,128]{3,2,1,0:T(8,128)S(1)}, f32[3,4,16,128]{3,2,1,0:T(8,128)}, u32[]{:S(2)}) copy-start(f32[3,4,16,128]{3,2,1,0:T(8,128)} %r_in.1) | copy-start | bytes 294916
  6.3 0.9 %copy-start.4 = (f32[3,4,16,128]{3,2,1,0:T(8,128)S(1)}, f32[3,4,16,128]{3,2,1,0:T(8,128)}, u32[]{:S(2)}) copy-start(f32[3,4,16,128]{3,2,1,0:T(8,128)} %p_in.1) | copy-start | bytes 294916
  7.2 0.8 %copy-start.5 = (f32[4,16,128]{2,1,0:T(8,128)S(1)}, f32[4,16,128]{2,1,0:T(8,128)}, u32[]{:S(2)}) copy-start(f32[4,16,128]{2,1,0:T(8,128)} %stiff.1) | copy-start | bytes 98308
where the time goes:
time: 37 us; the launch traced here: 36.6 us
  Pallas kernels  26.7 us (72%)
  local copies, waits for them, and re-layouts  7.29 us (20%)
  between operations  2.64 us (7%)
    pallas_call x1, Pallas kernels, on_device(): pl.pallas_call(functools.partial(kernel, nd, nb, levels), out_shape=(jax....  26.7 us
    unnamed x16, local copies, waits for them, and re-layouts  7.12 us

commit v1 on v0

--- a/solution.py
+++ b/solution.py
@@ -16,8 +16,9 @@
 
 def kernel(
     nd, nb, levels,
-    rhs, stiff, cpl, x_in, r_in, p_in, bk, beta, fc, bb,
+    rhs_h, stiff_h, cpl_h, x_h, r_h, p_h, bk, beta, fc, bb,
     x_out, r_out, b_out,
+    rhs, stiff, cpl, x_in, r_in, p_in, in_sems,
     pads, padl, flat, ysend, yrecv, csend, crecv, saved, bsend, brecv,
     r0, inv, img, target, solved, update,
     red, red2, rrecv, brecv2,
@@ -47,6 +48,14 @@
         stride = 1 << level
         return bud + stride * (1 - 2 * (lax.rem(bud // stride, 2)))
 
+    loads = {}
+    for i, (name, src, dst) in enumerate((
+        ("cpl", cpl_h, cpl), ("stiff", stiff_h, stiff), ("x", x_h, x_in),
+        ("p", p_h, p_in), ("r", r_h, r_in), ("rhs", rhs_h, rhs),
+    )):
+        loads[name] = pltpu.make_async_copy(src, dst, in_sems.at[i])
+        loads[name].start()
+
     pads[...] = jnp.zeros(pads.shape, pads.dtype)
     padl[...] = jnp.zeros(padl.shape, padl.dtype)
     yrecv[...] = jnp.zeros(yrecv.shape, yrecv.dtype)
@@ -70,6 +79,8 @@
         def _(side=side):
             greet(dom + side[0], bud + side[1])
 
+    for name in ("cpl", "stiff", "x"):
+        loads[name].wait()
     me_failed = jnp.full((1, ny, nz), fc[0], jnp.int32) == bud
     bit_here = jnp.full((1, ny, nz), bb[0], jnp.int32)
 
@@ -155,14 +166,14 @@
                         for dz in range(3):
                             o = (dx * 3 + dy) * 3 + dz
                             for a in range(3):
-                                term = cpl[o * 9 + a * 3 + b] * w
+                                term = cpl[a, b, o] * w
                                 acc[dz][a] = term if acc[dz][a] is None else acc[dz][a] + term
             for a in range(3):
                 before = jnp.where(lane == 0, 0.0, pltpu.roll(acc[0][a], 1, 2))
                 after = jnp.where(lane == nz - 1, 0.0, pltpu.roll(acc[2][a], nz - 1, 2))
                 out[a, pl.ds(x, step)] = acc[1][a] + before + after
 
-    centre = [cpl[13 * 9 + a * 3 + a] for a in range(3)]
+    centre = [cpl[a, a, 13] for a in range(3)]
 
     for a in range(3):
         scaled = jnp.where(me_failed, 0.0, x_in[a] * stiff[...])
@@ -192,6 +203,7 @@
             value = jnp.where(bit_here == l, buf[l, w, a], value)
         return value
 
+    loads["p"].wait()
     for l in range(levels):
         fetch[1][l].wait_recv()
     for a in range(3):
@@ -202,6 +214,8 @@
         pads[1, a, 1:nx + 1, Y0:Y0 + ny, :] = u0
     pack(1)
     send_halo(1)
+    for name in ("r", "rhs"):
+        loads[name].wait()
     for l in range(levels):
         fetch[0][l].wait_recv()
     for a in range(3):
@@ -216,10 +230,6 @@
         pads[2, a, 1:nx + 1, Y0:Y0 + ny, :] = a0
     pack(2)
     send_halo(2)
-    for l in range(levels):
-        keep[0][l].start()
-    for l in range(levels):
-        keep[1][l].start()
 
     take_halo(1)
     apply(pads.at[1], img.at[0])
@@ -231,8 +241,9 @@
     send_halo(3)
     for a in range(3):
         bsend[2, a] = flat[3, a] / stiff[...]
-    for l in range(levels):
-        keep[2][l].start()
+    for w in range(3):
+        for l in range(levels):
+            keep[w][l].start()
 
     take_halo(2)
     apply(pads.at[2], img.at[1])
@@ -358,9 +369,16 @@
             jax.ShapeDtypeStruct(field, f32),
             jax.ShapeDtypeStruct((2,) + field, f32),
         ),
-        in_specs=[vmem, vmem, smem, vmem, vmem, vmem, vmem, smem, smem, smem],
+        in_specs=[pl.BlockSpec(memory_space=pltpu.HBM)] * 7 + [smem] * 3,
         out_specs=(vmem, vmem, vmem),
         scratch_shapes=[
+            pltpu.VMEM(field, f32),
+            pltpu.VMEM((nx, ny, nz), f32),
+            pltpu.SMEM((3, 3, 27), f32),
+            pltpu.VMEM(field, f32),
+            pltpu.VMEM(field, f32),
+            pltpu.VMEM(field, f32),
+            dma((6,)),
             pltpu.VMEM((4, 3, nx + 2, ny + 2 * Y0, nz), f32),
             pltpu.VMEM((3, nx + 2, ny + 2 * Y0, nz), f32),
             pltpu.VMEM((4,) + field, f32),
@@ -390,7 +408,9 @@
         compiler_params=pltpu.CompilerParams(
             collective_id=0, has_side_effects=True, vmem_limit_bytes=40 * 1024 * 1024
         ),
-    )(rhs, stiff, coupling.reshape(-1), x_in, r_in, p_in, backup_in, beta, fc, bb)
+    )(*[pltpu.with_memory_space_constraint(v, pltpu.HBM) for v in (
+        rhs, stiff, jnp.transpose(coupling, (1, 2, 0)), x_in, r_in, p_in, backup_in
+    )], beta, fc, bb)
 
 
 def solution(mesh):

time: 37 us -> 31.1 us (0.84)
  local copies, waits for them, and re-layouts: 7.29 us -> 1.96 us
    unnamed x16 -> x3, local copies, waits for them, and re-layouts: 7.12 us -> 1.96 us
where the time goes in v1:
time: 31.1 us; the launch traced here: 30.9 us
  Pallas kernels  26.4 us (85%)
  between operations  2.58 us (8%)
  local copies, waits for them, and re-layouts  1.96 us (6%)
    pallas_call x1, Pallas kernels, on_device(): pl.pallas_call(functools.partial(kernel, nd, nb, levels), out_shape=(jax....  26.4 us
    unnamed x3, local copies, waits for them, and re-layouts  1.96 us

profile of v1, /device:TPU:0, one launch (start us, length us, event | category | flops | bytes accessed | tf_op | source)
XLA Modules:
  0.0 30.9 jit_solution(9253504586033159744)
XLA Ops:
  2.6 26.4 %shard_map.121 = (f32[3,4,16,128]{3,2,1,0:T(8,128)S(1)}, f32[3,4,16,128]{3,2,1,0:T(8,128)S(1)}, f32[2,3,4,16,128]{4,3,2,1,0:T(8,128)S(1)}) custom-call(f32[3,4,16,128]{3,2,1,0:T(8,128)} %rhs_h.1, f32[4,16,128]{2,1,0:T(8,128)} %stiff_h.1, f32[3,3,27]{2,1,0:T(4,128)} %bitcast.1, f32[3,4,16,128]{3,2,1,0:T(8,128)} %x_h.1, f32[3,4,16,128]{3,2,1,0:T(8,128)} %r_h.1, ...), custom_call_target="tpu_custom_call" | custom-call | tf_op jit(solution)/shard_map/pallas_call | solution.py:365
  29.0 0.6 %copy.19 = f32[3,4,16,128]{3,2,1,0:T(8,128)} copy(f32[3,4,16,128]{3,2,1,0:T(8,128)S(1)} %get-tuple-element.6) | data formatting | bytes 196608
  29.6 0.6 %copy.20 = f32[3,4,16,128]{3,2,1,0:T(8,128)} copy(f32[3,4,16,128]{3,2,1,0:T(8,128)S(1)} %get-tuple-element.7) | data formatting | bytes 196608
  30.3 0.7 %copy.21 = f32[2,3,4,16,128]{4,3,2,1,0:T(8,128)} copy(f32[2,3,4,16,128]{4,3,2,1,0:T(8,128)S(1)} %get-tuple-element.8) | data formatting | bytes 393216

commit v2 on v1

--- a/solution.py
+++ b/solution.py
@@ -17,11 +17,11 @@
 def kernel(
     nd, nb, levels,
     rhs_h, stiff_h, cpl_h, x_h, r_h, p_h, bk, beta, fc, bb,
-    x_out, r_out, b_out,
+    x_out, r0, bsend, b_out, img, s_out, coef,
     rhs, stiff, cpl, x_in, r_in, p_in, in_sems,
-    pads, padl, flat, ysend, yrecv, csend, crecv, saved, bsend, brecv,
-    r0, inv, img, target, solved, update,
-    red, red2, rrecv, brecv2,
+    pads, padl, flat, ysend, yrecv, csend, crecv, saved, brecv,
+    inv, img3, target, solved, update,
+    red, red1, red2, rrecv, brecv2,
     hs, hr, ss, sr, bs, br, d1s, d1r, d2s, d2r,
 ):
     nx, ny, nz = stiff.shape
@@ -48,6 +48,7 @@
         stride = 1 << level
         return bud + stride * (1 - 2 * (lax.rem(bud // stride, 2)))
 
+    coef[...] = jnp.zeros(coef.shape, coef.dtype)
     loads = {}
     for i, (name, src, dst) in enumerate((
         ("cpl", cpl_h, cpl), ("stiff", stiff_h, stiff), ("x", x_h, x_in),
@@ -114,19 +115,19 @@
             dst = crecv.at[e, i]
         return remote(src, dst, hs.at[e, i], hr.at[e, i], dom + sx, bud + sy)
 
-    def pack(e):
+    def pack(e, corners=None):
         for c in range(3):
-            for x in range(nx):
+            for x in range(nx if corners is not True else 0):
                 row = c * nx + x
                 ysend[e, 0, row:row + 1, :] = flat[e, c, x, 0:1, :]
                 ysend[e, 1, row:row + 1, :] = flat[e, c, x, ny - 1:ny, :]
             for i, (sx, sy) in enumerate(SIDES):
-                if sx != 0 and sy != 0:
+                if sx != 0 and sy != 0 and corners is not False:
                     y = ny - 1 if sy > 0 else 0
                     csend[e, i, c:c + 1, :] = flat[e, c, nx - 1 if sx > 0 else 0, y:y + 1, :]
 
-    def send_halo(e):
-        for side in SIDES:
+    def send_halo(e, sides=SIDES):
+        for side in sides:
             @pl.when(has(side))
             def _(side=side):
                 halo_copies(e, 0, side).start()
@@ -186,10 +187,12 @@
     beside_y = jnp.where(bud > 0, 1, 0) + jnp.where(bud < nb - 1, 1, 0)
     pl.semaphore_wait(barrier, nb - 1 + nd - 1 + beside_x * beside_y)
 
-    fetch = [[remote(bk.at[w], saved.at[l, w], ss.at[l, w], sr.at[l, w], dom, flip(l))
-              for l in range(levels)] for w in range(2)]
-    for l in range(levels):
-        fetch[1][l].start()
+    pieces = [(0, pl.ds(0, nx)), (1, pl.ds(0, 1)), (1, pl.ds(nx - 1, 1)), (1, pl.ds(1, nx - 2))]
+    fetch = [[remote(bk.at[w, :, x], saved.at[l, w, :, x], ss.at[l, i], sr.at[l, i], dom, flip(l))
+              for l in range(levels)] for i, (w, x) in enumerate(pieces)]
+    for i in (1, 2, 3):
+        for l in range(levels):
+            fetch[i][l].start()
     send_halo(0)
     for l in range(levels):
         fetch[0][l].start()
@@ -203,17 +206,32 @@
             value = jnp.where(bit_here == l, buf[l, w, a], value)
         return value
 
+    def start_field(x):
+        for a in range(3):
+            got = saved[0, 1, a, x]
+            for l in range(1, levels):
+                got = jnp.where(bit_here == l, saved[l, 1, a, x], got)
+            p0 = jnp.where(me_failed, got, p_in[a, x])
+            bsend[0, a, x] = p0
+            u0 = p0 * stiff[x]
+            flat[1, a, x] = u0
+            pads[1, a, x.start + 1:x.stop + 1, Y0:Y0 + ny, :] = u0
+
     loads["p"].wait()
+    for i in (1, 2):
+        for l in range(levels):
+            fetch[i][l].wait_recv()
+    start_field(slice(0, 1))
+    start_field(slice(nx - 1, nx))
+    pack(1, True)
+    send_halo(1, [s for s in SIDES if s[0] != 0])
     for l in range(levels):
-        fetch[1][l].wait_recv()
-    for a in range(3):
-        p0 = jnp.where(me_failed, pick(saved, 1, a), p_in[a])
-        bsend[0, a] = p0
-        u0 = p0 * stiff[...]
-        flat[1, a] = u0
-        pads[1, a, 1:nx + 1, Y0:Y0 + ny, :] = u0
-    pack(1)
-    send_halo(1)
+        fetch[3][l].wait_recv()
+    start_field(slice(1, nx - 1))
+    pack(1, False)
+    send_halo(1, [s for s in SIDES if s[0] == 0])
+    for l in range(levels):
+        keep[0][l].start()
     for name in ("r", "rhs"):
         loads[name].wait()
     for l in range(levels):
@@ -241,14 +259,14 @@
     send_halo(3)
     for a in range(3):
         bsend[2, a] = flat[3, a] / stiff[...]
-    for w in range(3):
+    for w in (1, 2):
         for l in range(levels):
             keep[w][l].start()
 
     take_halo(2)
     apply(pads.at[2], img.at[1])
     take_halo(0)
-    apply(pads.at[0], img.at[3])
+    apply(pads.at[0], img3)
     take_halo(3)
     apply(pads.at[3], img.at[2])
 
@@ -269,7 +287,11 @@
     red[5:6, :] = dot(lambda a: flat[3, a] * img[1, a])
     red[6:7, :] = dot(lambda a: flat[3, a] * img[2, a])
 
-    first = [remote(red, rrecv.at[j - 1], d1s.at[j - 1], d1r.at[j - 1], lax.rem(dom + j, nd), bud)
+    rows = lax.broadcasted_iota(jnp.int32, (8, nz), 0)
+    diagonal = rows == lax.broadcasted_iota(jnp.int32, (8, nz), 1)
+    each = jnp.sum(red[...], axis=1, keepdims=True)
+    red1[...] = jnp.sum(jnp.where(diagonal, each, 0.0), axis=0, keepdims=True)
+    first = [remote(red1, rrecv.at[j - 1], d1s.at[j - 1], d1r.at[j - 1], lax.rem(dom + j, nd), bud)
              for j in range(1, nd)]
     for c in first:
         c.start()
@@ -279,17 +301,17 @@
     ratio_value = centre_value / half_width
     weight = 1.0 / ratio_value
     for a in range(3):
-        t = target[a] - img[3, a] * stiff[...]
+        t = target[a] - img3[a] * stiff[...]
         d = inv[a] * t / centre_value
         target[a] = t
         update[a] = d
         solved[a] = d
         padl[a, 1:nx + 1, Y0:Y0 + ny, :] = d * stiff[...]
     for sweep in range(SWEEPS - 1):
-        apply(padl, img.at[3])
+        apply(padl, img3)
         weight_next = 1.0 / (2.0 * ratio_value - weight)
         for a in range(3):
-            remain = target[a] - img[3, a] * stiff[...]
+            remain = target[a] - img3[a] * stiff[...]
             d = weight_next * weight * update[a] + (2.0 * weight_next / half_width) * (inv[a] * remain)
             y = solved[a] + d
             update[a] = d
@@ -300,7 +322,7 @@
 
     for c in first:
         c.wait_recv()
-    total = red[...]
+    total = red1[...]
     for j in range(nd - 1):
         total = total + rrecv[j]
     red2[...] = total
@@ -311,14 +333,12 @@
     for w in range(3):
         for l in range(levels):
             keep[w][l].wait_recv()
-    for a in range(3):
-        b_out[0, a] = pick(brecv, 0, a)
     for c in second:
         c.wait_recv()
     total = red2[...]
     for j in range(nb - 1):
         total = total + brecv2[j]
-    sums = jnp.sum(total, axis=1, keepdims=True)
+    sums = jnp.sum(jnp.where(diagonal, jnp.broadcast_to(total, (8, nz)), 0.0), axis=1, keepdims=True)
     g0, c0, e0, f0, h0, h1, h2 = [jnp.broadcast_to(sums[j:j + 1], (1, nz)) for j in range(7)]
     alpha0 = g0 / c0
     g1 = g0 - 2.0 * alpha0 * e0 + alpha0 * alpha0 * f0
@@ -328,29 +348,47 @@
         + 2.0 * beta0 * (e0 - alpha0 * f0) + beta0 * beta0 * c0
     )
     alpha1 = g1 / c1
-    alpha0, beta0, alpha1 = alpha0[None], beta0[None], alpha1[None]
-    for a in range(3):
-        p0 = bsend[0, a]
-        p1 = bsend[1, a] - alpha0 * bsend[2, a] + beta0 * p0
-        x0 = jnp.where(me_failed, solved[a], x_in[a])
-        x_out[a] = x0 + alpha0 * p0 + alpha1 * p1
-        t0 = img[0, a]
-        q1 = img[1, a] - alpha0 * img[2, a] + beta0 * t0
-        r_out[a] = r0[a] - stiff[...] * (alpha0 * t0 + alpha1 * q1)
-        b_out[1, a] = (
-            pick(brecv, 1, a) - alpha0 * pick(brecv, 2, a) + beta0 * pick(brecv, 0, a)
-        )
-
+    coef[0:1, :] = alpha0
+    coef[1:2, :] = beta0
+    coef[2:3, :] = alpha1
+    for a in range(3):
+        x_out[a] = jnp.where(me_failed, solved[a], x_in[a])
+        for w in range(3):
+            b_out[w, a] = pick(brecv, w, a)
+
+    s_out[...] = stiff[...]
     for e in range(4):
         end_halo(e)
-    for w in range(2):
-        for l in range(levels):
-            fetch[w][l].wait_send()
+    for i in range(4):
+        for l in range(levels):
+            fetch[i][l].wait_send()
     for w in range(3):
         for l in range(levels):
             keep[w][l].wait_send()
     for c in first + second:
         c.wait_send()
+
+
+def finish(x0, r0, own, other, img, stiff, coef, x_out, r_out, b_out, xs, rs, bs, sems):
+    copies = [pltpu.make_async_copy(other.at[0], b_out.at[0], sems.at[9])]
+    copies[0].start()
+    alpha0, beta0, alpha1 = coef[0:1, :], coef[1:2, :], coef[2:3, :]
+    alpha0, beta0, alpha1 = alpha0[None], beta0[None], alpha1[None]
+    for a in range(3):
+        bs[a] = other[1, a] - alpha0 * other[2, a] + beta0 * other[0, a]
+        p0 = own[0, a]
+        p1 = own[1, a] - alpha0 * own[2, a] + beta0 * p0
+        xs[a] = x0[a] + alpha0 * p0 + alpha1 * p1
+        t0 = img[0, a]
+        q1 = img[1, a] - alpha0 * img[2, a] + beta0 * t0
+        rs[a] = r0[a] - stiff[...] * (alpha0 * t0 + alpha1 * q1)
+        for i, (src, dst) in enumerate((
+            (bs.at[a], b_out.at[1, a]), (xs.at[a], x_out.at[a]), (rs.at[a], r_out.at[a]),
+        )):
+            copies.append(pltpu.make_async_copy(src, dst, sems.at[a * 3 + i]))
+            copies[-1].start()
+    for c in copies:
+        c.wait()
 
 
 def on_device(nd, nb, rhs, stiff, coupling, x_in, r_in, p_in, backup_in, beta, fc, bb):
@@ -360,17 +398,22 @@
     rows = -(-3 * nx // 8) * 8
     vmem = pl.BlockSpec(memory_space=pltpu.VMEM)
     smem = pl.BlockSpec(memory_space=pltpu.SMEM)
+    hbm = pl.BlockSpec(memory_space=pltpu.HBM)
     field = (3, nx, ny, nz)
     dma = pltpu.SemaphoreType.DMA
-    return pl.pallas_call(
+    parts = pl.pallas_call(
         functools.partial(kernel, nd, nb, levels),
         out_shape=(
-            jax.ShapeDtypeStruct(field, f32),
-            jax.ShapeDtypeStruct(field, f32),
-            jax.ShapeDtypeStruct((2,) + field, f32),
+            pltpu.VMEM(field, f32),
+            pltpu.VMEM(field, f32),
+            pltpu.VMEM((3,) + field, f32),
+            pltpu.VMEM((3,) + field, f32),
+            pltpu.VMEM((3,) + field, f32),
+            pltpu.VMEM((nx, ny, nz), f32),
+            pltpu.VMEM((8, nz), f32),
         ),
-        in_specs=[pl.BlockSpec(memory_space=pltpu.HBM)] * 7 + [smem] * 3,
-        out_specs=(vmem, vmem, vmem),
+        in_specs=[hbm] * 7 + [smem] * 3,
+        out_specs=(vmem,) * 7,
         scratch_shapes=[
             pltpu.VMEM(field, f32),
             pltpu.VMEM((nx, ny, nz), f32),
@@ -387,20 +430,19 @@
             pltpu.VMEM((4, 8, 8, nz), f32),
             pltpu.VMEM((4, 8, 8, nz), f32),
             pltpu.VMEM((levels, 2) + field, f32),
-            pltpu.VMEM((3,) + field, f32),
             pltpu.VMEM((levels, 3) + field, f32),
             pltpu.VMEM(field, f32),
             pltpu.VMEM(field, f32),
-            pltpu.VMEM((4,) + field, f32),
             pltpu.VMEM(field, f32),
             pltpu.VMEM(field, f32),
             pltpu.VMEM(field, f32),
             pltpu.VMEM((8, nz), f32),
-            pltpu.VMEM((8, nz), f32),
-            pltpu.VMEM((nd - 1, 8, nz), f32),
-            pltpu.VMEM((nb - 1, 8, nz), f32),
+            pltpu.VMEM((1, nz), f32),
+            pltpu.VMEM((1, nz), f32),
+            pltpu.VMEM((nd - 1, 1, nz), f32),
+            pltpu.VMEM((nb - 1, 1, nz), f32),
             dma((4, 8)), dma((4, 8)),
-            dma((levels, 2)), dma((levels, 2)),
+            dma((levels, 4)), dma((levels, 4)),
             dma((levels, 3)), dma((levels, 3)),
             dma((nd - 1,)), dma((nd - 1,)),
             dma((nb - 1,)), dma((nb - 1,)),
@@ -411,6 +453,18 @@
     )(*[pltpu.with_memory_space_constraint(v, pltpu.HBM) for v in (
         rhs, stiff, jnp.transpose(coupling, (1, 2, 0)), x_in, r_in, p_in, backup_in
     )], beta, fc, bb)
+    return pl.pallas_call(
+        finish,
+        out_shape=(
+            pltpu.HBM(field, f32), pltpu.HBM(field, f32), pltpu.HBM((2,) + field, f32),
+        ),
+        in_specs=[vmem] * 7,
+        out_specs=(hbm, hbm, hbm),
+        scratch_shapes=[
+            pltpu.VMEM(field, f32), pltpu.VMEM(field, f32), pltpu.VMEM(field, f32), dma((10,)),
+        ],
+        compiler_params=pltpu.CompilerParams(vmem_limit_bytes=8 * 1024 * 1024),
+    )(*parts)
 
 
 def solution(mesh):

time: 31.1 us -> 29.5 us (0.949)
  local copies, waits for them, and re-layouts: 1.96 us -> 0 us
  Pallas kernels: 26.4 us -> 26.8 us
    unnamed x3 -> x0, local copies, waits for them, and re-layouts: 1.96 us -> none
    pallas_call x1 -> x2, Pallas kernels: 26.4 us -> 26.8 us  [the longest x1 25.9 us: on_device(): pl.pallas_call(functools.partial(kernel, nd, nb, levels), out_shape=(pltp...]
where the time goes in v2:
time: 29.5 us; the launch traced here: 29.3 us
  Pallas kernels  26.8 us (91%)
  between operations  2.58 us (9%)
    pallas_call x1, Pallas kernels, on_device(): pl.pallas_call(functools.partial(kernel, nd, nb, levels), out_shape=(pltp...  25.9 us
    pallas_call x1, Pallas kernels, on_device(): pl.pallas_call(finish, out_shape=(pltpu.HBM(field, f32), pltpu.HBM(field,...  0.82 us

profile of v2, /device:TPU:0, one launch (start us, length us, event | category | flops | bytes accessed | tf_op | source)
XLA Modules:
  0.0 29.3 jit_solution(3434170584556462706)
XLA Ops:
  2.6 25.9 %shard_map.121 = (f32[3,4,16,128]{3,2,1,0:T(8,128)S(1)}, f32[3,4,16,128]{3,2,1,0:T(8,128)S(1)}, f32[3,3,4,16,128]{4,3,2,1,0:T(8,128)S(1)}, f32[3,3,4,16,128]{4,3...) custom-call(f32[3,4,16,128]{3,2,1,0:T(8,128)} %rhs_h.1, ...), custom_call_target="tpu_custom_call" | custom-call | tf_op jit(solution)/shard_map/pallas_call | solution.py:404
  28.5 0.8 %shard_map.122 = (f32[3,4,16,128]{3,2,1,0:T(8,128)}, f32[3,4,16,128]{3,2,1,0:T(8,128)}, f32[2,3,4,16,128]{4,3,2,1,0:T(8,128)}) custom-call(f32[3,4,16,128]{3,2,1,0:T(8,128)S(1)} %get-tuple-element.10.x0, f32[3,4,16,128]{3,2,1,0:T(8,128)S(1)} %get-tuple-element.11.r0, f32[3,3,4,16,128]{4,3,2,1,0:T(8,128)S(1)} %get-tuple-element.12.own, ...), custom_call_target="tpu_custom_call" | custom-call | tf_op jit(solution)/shard_map/pallas_call | solution.py:456

commit v3 on v2

--- a/solution.py
+++ b/solution.py
@@ -57,8 +57,13 @@
         loads[name] = pltpu.make_async_copy(src, dst, in_sems.at[i])
         loads[name].start()
 
-    pads[...] = jnp.zeros(pads.shape, pads.dtype)
-    padl[...] = jnp.zeros(padl.shape, padl.dtype)
+    for pad in [pads.at[e] for e in range(4)] + [padl]:
+        face = jnp.zeros((3, ny + 2 * Y0, nz), pad.dtype)
+        pad[:, 0] = face
+        pad[:, nx + 1] = face
+        rim = jnp.zeros((3, nx, Y0, nz), pad.dtype)
+        pad[:, 1:nx + 1, 0:Y0, :] = rim
+        pad[:, 1:nx + 1, Y0 + ny:ny + 2 * Y0, :] = rim
     yrecv[...] = jnp.zeros(yrecv.shape, yrecv.dtype)
     crecv[...] = jnp.zeros(crecv.shape, crecv.dtype)
 
@@ -267,9 +272,6 @@
     apply(pads.at[2], img.at[1])
     take_halo(0)
     apply(pads.at[0], img3)
-    take_halo(3)
-    apply(pads.at[3], img.at[2])
-
     def dot(*terms):
         total = None
         for a in range(3):
@@ -285,6 +287,8 @@
     red[3:4, :] = dot(lambda a: flat[3, a] * img[0, a])
     red[4:5, :] = dot(lambda a: flat[2, a] * img[1, a])
     red[5:6, :] = dot(lambda a: flat[3, a] * img[1, a])
+    take_halo(3)
+    apply(pads.at[3], img.at[2])
     red[6:7, :] = dot(lambda a: flat[3, a] * img[2, a])
 
     rows = lax.broadcasted_iota(jnp.int32, (8, nz), 0)
@@ -333,6 +337,13 @@
     for w in range(3):
         for l in range(levels):
             keep[w][l].wait_recv()
+    for a in range(3):
+        x_out[a] = jnp.where(me_failed, solved[a], x_in[a])
+        for w in range(3):
+            b_out[w, a] = pick(brecv, w, a)
+    s_out[...] = stiff[...]
+    for e in range(4):
+        end_halo(e)
     for c in second:
         c.wait_recv()
     total = red2[...]
@@ -351,14 +362,7 @@
     coef[0:1, :] = alpha0
     coef[1:2, :] = beta0
     coef[2:3, :] = alpha1
-    for a in range(3):
-        x_out[a] = jnp.where(me_failed, solved[a], x_in[a])
-        for w in range(3):
-            b_out[w, a] = pick(brecv, w, a)
-
-    s_out[...] = stiff[...]
-    for e in range(4):
-        end_halo(e)
+
     for i in range(4):
         for l in range(levels):
             fetch[i][l].wait_send()

time: 29.5 us -> 29.5 us (level)
  no operation moved by 1% of the time
where the time goes in v3:
time: 29.5 us; the launch traced here: 29.3 us
  Pallas kernels  26.7 us (91%)
  between operations  2.58 us (9%)
    pallas_call x1, Pallas kernels, on_device(): pl.pallas_call(functools.partial(kernel, nd, nb, levels), out_shape=(pltp...  25.9 us
    pallas_call x1, Pallas kernels, on_device(): pl.pallas_call(finish, out_shape=(pltpu.HBM(field, f32), pltpu.HBM(field,...  0.82 us

profile of v3, /device:TPU:0, one launch (start us, length us, event | category | flops | bytes accessed | tf_op | source)
XLA Modules:
  0.0 29.3 jit_solution(15009456051717485711)
XLA Ops:
  2.6 25.9 %shard_map.121 = (f32[3,4,16,128]{3,2,1,0:T(8,128)S(1)}, f32[3,4,16,128]{3,2,1,0:T(8,128)S(1)}, f32[3,3,4,16,128]{4,3,2,1,0:T(8,128)S(1)}, f32[3,3,4,16,128]{4,3...) custom-call(f32[3,4,16,128]{3,2,1,0:T(8,128)} %rhs_h.1, ...), custom_call_target="tpu_custom_call" | custom-call | tf_op jit(solution)/shard_map/pallas_call | solution.py:408
  28.5 0.8 %shard_map.122 = (f32[3,4,16,128]{3,2,1,0:T(8,128)}, f32[3,4,16,128]{3,2,1,0:T(8,128)}, f32[2,3,4,16,128]{4,3,2,1,0:T(8,128)}) custom-call(f32[3,4,16,128]{3,2,1,0:T(8,128)S(1)} %get-tuple-element.10.x0, f32[3,4,16,128]{3,2,1,0:T(8,128)S(1)} %get-tuple-element.11.r0, f32[3,3,4,16,128]{4,3,2,1,0:T(8,128)S(1)} %get-tuple-element.12.own, ...), custom_call_target="tpu_custom_call" | custom-call | tf_op jit(solution)/shard_map/pallas_call | solution.py:460
